TPU v7x, 512 devices: a whole 4x8x8 slice. The times are simulated.
512 devices in a mesh: leaf: 64 (over y_lo, z, core), blk: 8 (over y_hi, x).
Axes of the slice: x: 4, y: 8 (y_hi: 2, y_lo: 4; y = y_hi * 4 + y_lo), z: 8, core: 2. Of those that a mesh axis runs over, the one named last changes fastest.
Arguments:
- leaf_rows: bfloat16 [128, 8, 512, 512], P('leaf', None, 'blk'), may hold values from -2 to 2
- leaf_weight: bfloat16 [128, 8, 512], P('leaf', None, 'blk'), may hold values from 0.25 to 4
- branching: int32 [128], P('leaf'), may hold values from 1 to 8, as said below
- sibling: int32 [64, 2], P('leaf'), may hold values from 0 to 1, each once within a row
- node_block: bfloat16 [512, 128, 512], P('blk', 'leaf'), may hold values from -6 to 6
- na_rows: bfloat16 [262144, 512], P(('leaf', 'blk')), may hold values from -2 to 2
- na_weight: bfloat16 [262144], P(('leaf', 'blk')), may hold values from 0.25 to 4
- na_route: int32 [262144, 1], P(('leaf', 'blk')), may hold values from 0 to 127; in each aligned block of 512 rows (0 to 511, 512 to 1023, ...) at most 6 rows name the same one
Outputs:
- node_schur: float32 [512, 128, 512], P('blk', 'leaf')
- merged: float32 [512, 128, 512], P('blk', 'leaf')
Inputs may be any that keep to these rules, and one draw needn't show every extreme that they name: `branching`: some node has exactly 8 children. `sibling`: each row is a permutation. `na_route`: within the rows of one device, no node is named by more than 6 rows, a bound that some block reaches.
All inputs are finite; a program needn't handle non-finite values.
Results may differ from a plain program's by a relative error of at most 0.0012.
Values may be sent and summed in bfloat16 or wider, within the bound.
A program may use at most 64 MiB of HBM per device.

v0:
```python
import jax
import jax.numpy as jnp
from jax import lax
from jax.sharding import PartitionSpec as P


def from_partner(shard, axis, apart):
    return lax.ppermute(shard, axis, [(i, i ^ 1 << apart) for i in range(lax.axis_size(axis))])


def bucket_rows(route, rows, weight, total_nodes, capacity):
    count = route.shape[0]
    order = jnp.argsort(route, stable=True)
    sorted_route = route[order]
    first = jnp.searchsorted(sorted_route, sorted_route, side="left")
    position = jnp.arange(count, dtype=jnp.int32) - first
    slot = sorted_route * capacity + position
    width = rows.shape[1]
    filled = jnp.zeros((total_nodes * capacity, width), rows.dtype).at[slot].set(rows[order])
    weights = jnp.zeros((total_nodes * capacity,), weight.dtype).at[slot].set(weight[order])
    return (filled, weights)


def scale_rows(rows, weight, alive):
    factor = weight.astype(jnp.float32) * alive[:, :, None]
    return (rows.astype(jnp.float32) * factor[..., None]).astype(jnp.bfloat16)


def shards(leaf_rows, leaf_weight, branching, sibling, node_block, na_rows, na_weight, na_route):
    leaf_count = lax.axis_size("leaf")
    node_dev = leaf_rows.shape[0]
    most_children = leaf_rows.shape[1]
    state = leaf_rows.shape[3]
    na_dev = na_rows.shape[0]
    capacity = 3 * na_dev // (2 * leaf_count * node_dev)
    live = (jnp.arange(most_children, dtype=jnp.int32)[None, :] < branching[:, None]).astype(
        jnp.float32
    )
    filled, fill_weights = bucket_rows(
        na_route[:, 0], na_rows, na_weight, leaf_count * node_dev, capacity
    )
    got_rows, got_weights = (
        lax.all_to_all(
            filled.reshape(leaf_count, node_dev * capacity, state),
            "leaf",
            split_axis=0,
            concat_axis=0,
            tiled=True,
        ),
        lax.all_to_all(
            fill_weights.reshape(leaf_count, node_dev * capacity),
            "leaf",
            split_axis=0,
            concat_axis=0,
            tiled=True,
        ),
    )
    got_scaled = (got_rows.astype(jnp.float32) * got_weights.astype(jnp.float32)[..., None]).astype(
        jnp.bfloat16
    )
    got_scaled = got_scaled.reshape(leaf_count, node_dev, capacity, state)
    got_plain = got_rows.reshape(leaf_count, node_dev, capacity, state)
    scaled_leaf = scale_rows(leaf_rows, leaf_weight, live)
    sliced = scaled_leaf
    leaf_part = lax.psum_scatter(
        jnp.einsum("nbks,nbkt->snt", sliced, leaf_rows, preferred_element_type=jnp.float32),
        "blk",
        scatter_dimension=0,
        tiled=True,
    )
    sliced = got_scaled
    routed_part = lax.psum_scatter(
        jnp.einsum("incs,inct->snt", sliced, got_plain, preferred_element_type=jnp.float32),
        "blk",
        scatter_dimension=0,
        tiled=True,
    )
    total = leaf_part + routed_part
    node_schur = total + node_block.astype(jnp.float32)
    partner = from_partner(node_schur, "leaf", 0)
    matches = sibling[0][:, None] == jnp.arange(node_dev, dtype=jnp.int32)[None, :]
    picked = jnp.sum(jnp.where(matches[None, :, :, None], partner[:, None, :, :], 0.0), axis=2)
    merged = node_schur + picked
    return (node_schur, merged)


def solution(mesh):
    return jax.shard_map(
        shards,
        mesh=mesh,
        in_specs=(
            P("leaf", None, "blk", None),
            P("leaf", None, "blk"),
            P("leaf"),
            P("leaf", None),
            P("blk", "leaf", None),
            P(("leaf", "blk"), None),
            P(("leaf", "blk")),
            P(("leaf", "blk"), None),
        ),
        out_specs=(P("blk", "leaf", None), P("blk", "leaf", None)),
        check_vma=False,
    )
```

profile of v0, /device:TPU:1, one launch (start us, length us, event | category | flops | bytes accessed | tf_op | source)
XLA Modules:
  0.0 232.9 jit_solution(13615272857006359754)
XLA Ops:
  7.2 4.5 %sort.17 = (s32[512]{0:T(512)}, s32[512]{0:T(512)S(1)}) sort(s32[512]{0:T(512)} %bitcast.17, s32[512]{0:T(512)S(1)} %iota.22), dimensions={0}, to_apply=%region_1.2 | sort | flops 4608 | bytes 8192 | tf_op jit(solution)/shard_map/jit(argsort)/sort | solution.py:13
  11.7 3.6 %gather_fusion.1 = s32[512]{0:T(512)S(1)} fusion(s32[512]{0:T(512)} %bitcast.18, s32[1024]{0:T(1024)S(1)} %pad_clamp_fusion.1), kind=kCustom, calls=%fused_computation.1 | custom fusion | bytes 6144 | tf_op jit(solution)/shard_map/gather | solution.py:14
  15.3 35.9 %while.25 = (s32[]{:T(128)}, u32[512]{0:T(512)S(1)}, u32[512]{0:T(512)S(1)}, s32[512]{0:T(512)S(1)}, s32[]{:T(128)}, /*index=5*/s32[]{:T(128)}, s32[]{}) while((s32[]{:T(128)}, u32[512]{0:T(512)S(1)}, u32[512]{0:T(512)S(1)}, s32[512]{0:T(512)S(1)}, s32[]{:T(128)}, /*index=5*/s32[]{:T(128)}, s32[]{}) %tuple.45), condition=%wide.region_3.4_spmd.clone, body=%wide.region_2.3_spmd.clone.sunk | while | flops 10244 | bytes 40037 | solution.py:15
  15.4 3.5 %gather_fusion = s32[512]{0:T(512)S(1)} fusion(s32[512]{0:T(512)S(1)} %get-tuple-element.153, u32[1024]{0:T(1024)S(1)} %pad_clamp_fusion.3), kind=kCustom, calls=%fused_computation.clone.clone.1 | custom fusion | bytes 6144 | tf_op jit(solution)/shard_map/jit(searchsorted)/jit(_searchsorted_scan_impl)/vmap(jit(_searchsorted_scan_impl))/while/body/eval_jaxpr/gather | solution.py:15
  19.0 3.5 %gather_fusion = s32[512]{0:T(512)S(1)} fusion(s32[512]{0:T(512)S(1)} %get-tuple-element.153, u32[1024]{0:T(1024)S(1)} %pad_clamp_fusion.3), kind=kCustom, calls=%fused_computation.clone.clone.1 | custom fusion | bytes 6144 | tf_op jit(solution)/shard_map/jit(searchsorted)/jit(_searchsorted_scan_impl)/vmap(jit(_searchsorted_scan_impl))/while/body/eval_jaxpr/gather | solution.py:15
  22.6 3.5 %gather_fusion = s32[512]{0:T(512)S(1)} fusion(s32[512]{0:T(512)S(1)} %get-tuple-element.153, u32[1024]{0:T(1024)S(1)} %pad_clamp_fusion.3), kind=kCustom, calls=%fused_computation.clone.clone.1 | custom fusion | bytes 6144 | tf_op jit(solution)/shard_map/jit(searchsorted)/jit(_searchsorted_scan_impl)/vmap(jit(_searchsorted_scan_impl))/while/body/eval_jaxpr/gather | solution.py:15
  26.1 3.5 %gather_fusion = s32[512]{0:T(512)S(1)} fusion(s32[512]{0:T(512)S(1)} %get-tuple-element.153, u32[1024]{0:T(1024)S(1)} %pad_clamp_fusion.3), kind=kCustom, calls=%fused_computation.clone.clone.1 | custom fusion | bytes 6144 | tf_op jit(solution)/shard_map/jit(searchsorted)/jit(_searchsorted_scan_impl)/vmap(jit(_searchsorted_scan_impl))/while/body/eval_jaxpr/gather | solution.py:15
  29.7 3.5 %gather_fusion = s32[512]{0:T(512)S(1)} fusion(s32[512]{0:T(512)S(1)} %get-tuple-element.153, u32[1024]{0:T(1024)S(1)} %pad_clamp_fusion.3), kind=kCustom, calls=%fused_computation.clone.clone.1 | custom fusion | bytes 6144 | tf_op jit(solution)/shard_map/jit(searchsorted)/jit(_searchsorted_scan_impl)/vmap(jit(_searchsorted_scan_impl))/while/body/eval_jaxpr/gather | solution.py:15
  33.3 3.5 %gather_fusion = s32[512]{0:T(512)S(1)} fusion(s32[512]{0:T(512)S(1)} %get-tuple-element.153, u32[1024]{0:T(1024)S(1)} %pad_clamp_fusion.3), kind=kCustom, calls=%fused_computation.clone.clone.1 | custom fusion | bytes 6144 | tf_op jit(solution)/shard_map/jit(searchsorted)/jit(_searchsorted_scan_impl)/vmap(jit(_searchsorted_scan_impl))/while/body/eval_jaxpr/gather | solution.py:15
  36.9 3.5 %gather_fusion = s32[512]{0:T(512)S(1)} fusion(s32[512]{0:T(512)S(1)} %get-tuple-element.153, u32[1024]{0:T(1024)S(1)} %pad_clamp_fusion.3), kind=kCustom, calls=%fused_computation.clone.clone.1 | custom fusion | bytes 6144 | tf_op jit(solution)/shard_map/jit(searchsorted)/jit(_searchsorted_scan_impl)/vmap(jit(_searchsorted_scan_impl))/while/body/eval_jaxpr/gather | solution.py:15
  40.5 3.5 %gather_fusion = s32[512]{0:T(512)S(1)} fusion(s32[512]{0:T(512)S(1)} %get-tuple-element.153, u32[1024]{0:T(1024)S(1)} %pad_clamp_fusion.3), kind=kCustom, calls=%fused_computation.clone.clone.1 | custom fusion | bytes 6144 | tf_op jit(solution)/shard_map/jit(searchsorted)/jit(_searchsorted_scan_impl)/vmap(jit(_searchsorted_scan_impl))/while/body/eval_jaxpr/gather | solution.py:15
  44.1 3.5 %gather_fusion = s32[512]{0:T(512)S(1)} fusion(s32[512]{0:T(512)S(1)} %get-tuple-element.153, u32[1024]{0:T(1024)S(1)} %pad_clamp_fusion.3), kind=kCustom, calls=%fused_computation.clone.clone.1 | custom fusion | bytes 6144 | tf_op jit(solution)/shard_map/jit(searchsorted)/jit(_searchsorted_scan_impl)/vmap(jit(_searchsorted_scan_impl))/while/body/eval_jaxpr/gather | solution.py:15
  47.7 3.5 %gather_fusion = s32[512]{0:T(512)S(1)} fusion(s32[512]{0:T(512)S(1)} %get-tuple-element.153, u32[1024]{0:T(1024)S(1)} %pad_clamp_fusion.3), kind=kCustom, calls=%fused_computation.clone.clone.1 | custom fusion | bytes 6144 | tf_op jit(solution)/shard_map/jit(searchsorted)/jit(_searchsorted_scan_impl)/vmap(jit(_searchsorted_scan_impl))/while/body/eval_jaxpr/gather | solution.py:15
  51.3 3.5 %gather_fusion.2 = bf16[512]{0:T(512)(128)(2,1)S(1)} fusion(bf16[512]{0:T(512)(128)(2,1)S(1)} %copy-done.1, s32[1024]{0:T(1024)S(1)} %pad_clamp_fusion.1), kind=kCustom, calls=%fused_computation.3 | custom fusion | bytes 4096 | tf_op jit(solution)/shard_map/gather | solution.py:20
  54.8 3.8 %scatter_custom_fusion.1 = bf16[768]{0:T(1024)(128)(2,1)S(1)} fusion(s32[512]{0:T(512)S(1)} %compare_select_fusion, bf16[512]{0:T(512)(128)(2,1)S(1)} %gather_fusion.2, bf16[]{:T(256)} %constant.38.clone.1), kind=kCustom, calls=%fused_computation.26 | custom fusion | bytes 1538 | tf_op jit(solution)/shard_map/scatter | solution.py:20
  58.6 0.7 all_to_all.12
  59.3 15.4 %all-to-all-start.1 = ((bf16[64,1,12]{2,1,0:T(2,128)(2,1)}), bf16[64,1,12]{2,1,0:T(2,128)(2,1)S(1)}, u32[]{:S(2)}, u32[]{:S(2)}) async-start(bf16[64,1,12]{2,1,0:T(2,128)(2,1)} %all_to_all.12), calls=%async_computation.1 | async-start | bytes 65536 | tf_op jit(solution)/shard_map/all_to_all | solution.py:50
  74.7 4.9 %scatter_custom_fusion = bf16[768,512]{1,0:T(8,128)(2,1)S(1)} fusion(s32[512]{0:T(512)S(1)} %compare_select_fusion, bf16[512,512]{1,0:T(8,128)(2,1)S(1)} %copy-done, s32[1024]{0:T(1024)S(1)} %pad_clamp_fusion.1, bf16[]{:T(256)} %constant.38.clone.1), kind=kCustom, calls=%fused_computation.15 | custom fusion | bytes 786434 | tf_op jit(solution)/shard_map/scatter | solution.py:19
  79.7 1.2 reshape.71
  80.9 3.4 %all-to-all-done.1 = bf16[64,1,12]{2,1,0:T(2,128)(2,1)S(1)} async-done(((bf16[64,1,12]{2,1,0:T(2,128)(2,1)}), bf16[64,1,12]{2,1,0:T(2,128)(2,1)S(1)}, u32[]{:S(2)}, u32[]{:S(2)}) %all-to-all-start.1) | async-done | bytes 1568 | tf_op jit(solution)/shard_map/all_to_all | solution.py:50
  84.2 7.6 %all-to-all-start = ((bf16[64,12,512]{2,1,0:T(8,128)(2,1)}), bf16[64,12,512]{2,1,0:T(8,128)(2,1)S(1)}, u32[]{:S(2)}, u32[]{:S(2)}) async-start(bf16[64,12,512]{2,1,0:T(8,128)(2,1)} %reshape.71), calls=%async_computation | async-start | bytes 2097152 | tf_op jit(solution)/shard_map/all_to_all | solution.py:43
  92.0 2.3 fusion
  94.3 26.1 %all-to-all-done = bf16[64,12,512]{2,1,0:T(8,128)(2,1)S(1)} async-done(((bf16[64,12,512]{2,1,0:T(8,128)(2,1)}), bf16[64,12,512]{2,1,0:T(8,128)(2,1)S(1)}, u32[]{:S(2)}, u32[]{:S(2)}) %all-to-all-start) | async-done | bytes 786464 | tf_op jit(solution)/shard_map/all_to_all | solution.py:43
  120.7 0.4 copy.39
  121.2 0.4 copy.37
  121.6 0.7 copy-done.2
  122.3 2.1 bitcast_add_fusion
  124.5 94.0 %reduce-scatter.2.cloned.1.call-done = f32[64,2,512]{2,0,1:T(8,128)} async-done(((f32[512,2,512]{2,0,1:T(8,128)}), f32[64,2,512]{2,0,1:T(8,128)}) %reduce-scatter.2.cloned.1.call-update) | async-done | bytes 262160 | tf_op jit(solution)/shard_map/reduce_scatter | solution.py:65
  218.5 1.0 convert_add_fusion
  219.5 4.4 %collective-permute-start = (f32[64,2,512]{2,0,1:T(8,128)S(1)}, f32[64,2,512]{2,0,1:T(8,128)S(1)}, u32[]{:S(2)}, u32[]{:S(2)}) collective-permute-start(f32[64,2,512]{2,0,1:T(8,128)S(1)} %convert_add_fusion), channel_id=1, source_target_pairs={{0,8},{8,0},{16,24},{24,16},{32,40},{40,32},{48,56},{56,48},{64,72... | collective-permute-start | bytes 786440 | tf_op jit(solution)/shard_map/ppermute | solution.py:8
  224.0 0.9 copy.42
  225.2 0.9 copy.43
  (81 shorter events, 1.4 us)
Async XLA Ops:
  7.2 67.5 %copy-start = (bf16[512,512]{1,0:T(8,128)(2,1)S(1)}, bf16[512,512]{1,0:T(8,128)(2,1)}, u32[]{:S(2)}) copy-start(bf16[512,512]{1,0:T(8,128)(2,1)} %param.15) | copy-start | bytes 1572868
  15.3 35.9 %copy-start.1 = (bf16[512]{0:T(512)(128)(2,1)S(1)}, bf16[512]{0:T(512)(128)(2,1)}, u32[]{:S(2)}) copy-start(bf16[512]{0:T(512)(128)(2,1)} %param.16) | copy-start | bytes 3076
  59.3 24.9 %all-to-all-start.1 = ((bf16[64,1,12]{2,1,0:T(2,128)(2,1)}), bf16[64,1,12]{2,1,0:T(2,128)(2,1)S(1)}, u32[]{:S(2)}, u32[]{:S(2)}) async-start(bf16[64,1,12]{2,1,0:T(2,128)(2,1)} %all_to_all.12), calls=%async_computation.1 | async-start | bytes 65536 | tf_op jit(solution)/shard_map/all_to_all | solution.py:50
  79.7 12.2 %copy-start.6 = (s32[2]{0:T(128)S(1)}, s32[2]{0:T(128)}, u32[]{:S(2)}) copy-start(s32[2]{0:T(128)} %param.12) | copy-start | bytes 28
  79.7 12.2 %copy-start.4 = (bf16[2,8,64]{2,1,0:T(8,128)(2,1)S(1)}, bf16[2,8,64]{2,1,0:T(8,128)(2,1)}, u32[]{:S(2)}) copy-start(bf16[2,8,64]{2,1,0:T(8,128)(2,1)} %param.11) | copy-start | bytes 6148
  79.7 12.3 %copy-start.5 = (bf16[2,8,64,512]{3,2,1,0:T(8,128)(2,1)S(1)}, bf16[2,8,64,512]{3,2,1,0:T(8,128)(2,1)}, u32[]{:S(2)}) copy-start(bf16[2,8,64,512]{3,2,1,0:T(8,128)(2,1)} %param.10) | copy-start | bytes 3145732
  84.2 36.2 %all-to-all-start = ((bf16[64,12,512]{2,1,0:T(8,128)(2,1)}), bf16[64,12,512]{2,1,0:T(8,128)(2,1)S(1)}, u32[]{:S(2)}, u32[]{:S(2)}) async-start(bf16[64,12,512]{2,1,0:T(8,128)(2,1)} %reshape.71), calls=%async_computation | async-start | bytes 2097152 | tf_op jit(solution)/shard_map/all_to_all | solution.py:43
  91.8 126.7 %reduce-scatter.2.cloned.1.call-start = ((), (), s32[]{:S(2)}) async-start(), calls=%async_computation.3 | async-start | bytes 2359296 | tf_op jit(solution)/shard_map/reduce_scatter | solution.py:65
  120.7 1.6 copy-start.2
  124.4 94.0 %copy-start.3 = (bf16[64,2,512]{2,1,0:T(2,128)(2,1)S(1)}, bf16[64,2,512]{2,1,0:T(2,128)(2,1)}, u32[]{:S(2)}) copy-start(bf16[64,2,512]{2,1,0:T(2,128)(2,1)} %param.14) | copy-start | bytes 393220
  124.4 99.5 %copy-start.7 = (s32[1,2]{1,0:T(1,128)S(1)}, s32[1,2]{1,0:T(1,128)}, u32[]{:S(2)}) copy-start(s32[1,2]{1,0:T(1,128)} %param.13) | copy-start | bytes 28
  219.5 5.6 %collective-permute-start = (f32[64,2,512]{2,0,1:T(8,128)S(1)}, f32[64,2,512]{2,0,1:T(8,128)S(1)}, u32[]{:S(2)}, u32[]{:S(2)}) collective-permute-start(f32[64,2,512]{2,0,1:T(8,128)S(1)} %convert_add_fusion), channel_id=1, source_target_pairs={{0,8},{8,0},{16,24},{24,16},{32,40},{40,32},{48,56},{56,48},{64,72... | collective-permute-start | bytes 786440 | tf_op jit(solution)/shard_map/ppermute | solution.py:8
Sparse Core Ops, SparseCore 0:
  124.6 93.8 reduce-scatter.1
where the time goes:
time: 233 us
  waiting for transfers between devices  124 us (53%)
  local copies, waits for them, and re-layouts  56.1 us (24%)
  starting transfers between devices  27.4 us (12%)
  between operations  14.2 us (6%)
  other arithmetic  6.58 us (3%)
  matrix products  4.41 us (2%)
    reduce_scatter x1, waiting for transfers between devices, shards(): lax.psum_scatter(jnp.einsum('nbks,nbkt->snt', sliced, leaf_rows, preferre...  94 us
    gather x10, local copies, waits for them, and re-layouts, bucket_rows(): first = jnp.searchsorted(sorted_route, sorted_route, side='left')  34.9 us
    all_to_all x1, waiting for transfers between devices, shards(): lax.all_to_all(filled.reshape(leaf_count, node_dev * capacity, state), 'l...  26.1 us
    all_to_all x1, starting transfers between devices, shards(): lax.all_to_all(fill_weights.reshape(leaf_count, node_dev * capacity), 'le...  15.4 us
    all_to_all x1, starting transfers between devices, shards(): lax.all_to_all(filled.reshape(leaf_count, node_dev * capacity, state), 'l...  7.55 us
    scatter x1, local copies, waits for them, and re-layouts, bucket_rows(): jnp.zeros((total_nodes * capacity, width), rows.dtype).at[slot]  4.94 us
  transfers between devices with their start and end apart: 4, of which 4 were waited for; matrix products, arithmetic and copies ran while one was open for 4% of the time, Pallas kernels for 0%

commit v1 on v0

v1 whole, which is shorter than its diff:
```python
import functools

import jax
import jax.numpy as jnp
from jax import lax
from jax.experimental import pallas as pl
from jax.experimental.pallas import tpu as pltpu
from jax.sharding import PartitionSpec as P

MESH = pl.DeviceIdType.MESH
F32 = jnp.float32
BF16 = jnp.bfloat16
WIRE = jnp.float32
ROWS_Y, ROWS_Z, CORES = 4, 8, 2
SIZE_X, SIZE_YH = 4, 2
CAP = 6
GROUP = 8


def outer_sum(scaled, plain):
    return lax.dot_general(
        scaled, plain, (((0,), (0,)), ((), ())), preferred_element_type=F32
    )


def kernel(
    branching,
    sibling,
    leaf_rows,
    leaf_weight,
    node_block,
    na_rows,
    na_weight,
    na_route,
    schur_out,
    merged_out,
    packed,
    packed_w,
    got,
    got_w,
    part,
    half,
    xs,
    xr,
    ys,
    yr,
    pr,
    a_send,
    a_recv,
    w_send,
    w_recv,
    x_send,
    x_recv,
    y_send,
    y_recv,
    p_send,
    p_recv,
    own_sem,
):
    leaves = ROWS_Y * ROWS_Z * CORES
    me = lax.axis_index("leaf")
    blk = lax.axis_index("blk")
    core, at_z, at_y = me % CORES, (me // CORES) % ROWS_Z, me // (CORES * ROWS_Z)
    at_x, at_yh = blk % SIZE_X, blk // SIZE_X
    state = na_rows.shape[1]
    count = na_rows.shape[0]
    lanes = 128
    block = state // (SIZE_X * SIZE_YH)

    def peer(k):
        mixed = (k * 27) % leaves
        to_core = (core + mixed % CORES) % CORES
        to_z = (at_z + (mixed // CORES) % ROWS_Z) % ROWS_Z
        to_y = (at_y + mixed // (CORES * ROWS_Z)) % ROWS_Y
        return (to_y * ROWS_Z + to_z) * CORES + to_core

    def x_peer(dx):
        return at_yh * SIZE_X + (at_x + dx) % SIZE_X

    yh_peer = (1 - at_yh) * SIZE_X + at_x
    partner = (me // CORES) * CORES + (1 - core)

    barrier = pltpu.get_barrier_semaphore()

    def greet(k, carry):
        pl.semaphore_signal(barrier, inc=1, device_id={"leaf": peer(k)}, device_id_type=MESH)
        return carry

    lax.fori_loop(1, leaves, greet, 0)
    for dx in range(1, SIZE_X):
        pl.semaphore_signal(barrier, inc=1, device_id={"blk": x_peer(dx)}, device_id_type=MESH)
    pl.semaphore_signal(barrier, inc=1, device_id={"blk": yh_peer}, device_id_type=MESH)

    route = na_route[...]
    route_f = route.astype(F32)
    at_diag = lax.broadcasted_iota(jnp.int32, (lanes, lanes), 0) == lax.broadcasted_iota(
        jnp.int32, (lanes, lanes), 1
    )
    place = jnp.zeros((1, count), F32)
    for b in range(count // lanes):
        own = route_f[:, b * lanes : (b + 1) * lanes]
        column = jnp.sum(jnp.where(at_diag, own, 0.0), axis=1, keepdims=True)
        earlier = lax.broadcasted_iota(jnp.int32, (lanes, count), 0) + b * lanes
        later = lax.broadcasted_iota(jnp.int32, (lanes, count), 1)
        same = (column == route_f) & (earlier < later)
        place = place + jnp.sum(jnp.where(same, 1.0, 0.0), axis=0, keepdims=True)
    slot = (route % 2) * (leaves * GROUP) + (route // 2) * GROUP + place.astype(jnp.int32)
    weight = na_weight[...].astype(F32)

    span = 128
    spans = leaves * GROUP // span
    subs = span // GROUP
    rank = lax.broadcasted_iota(jnp.int32, (span, lanes), 0) % GROUP
    lane = lax.broadcasted_iota(jnp.int32, (span, lanes), 1)

    def bucket(q):
        def one(i, carry):
            first = q * (leaves * GROUP) + i * span
            index = lax.broadcasted_iota(jnp.int32, (span, count), 0) + first
            hit = index == slot
            pick = jnp.where(hit, 1.0, 0.0).astype(BF16)
            filled = jnp.dot(pick, na_rows[...], preferred_element_type=F32)
            tail = filled[:, 3 * lanes :]
            at = pl.ds(i * subs, subs)
            for c in range(3):
                moved = pltpu.roll(tail, CAP - 2 * c, 0)
                tile = jnp.where(rank < CAP, filled[:, c * lanes : (c + 1) * lanes], moved)
                packed[q, at, c] = tile.reshape(subs, GROUP, lanes).astype(BF16)
            slot_w = jnp.sum(jnp.where(hit, weight, 0.0), axis=1, keepdims=True)
            spread = jnp.where(rank == lane, slot_w, 0.0).reshape(subs, GROUP, lanes)
            packed_w[q, at] = jnp.sum(spread, axis=1, keepdims=True)
            return carry

        lax.fori_loop(0, spans, one, 0)

    for q in range(2):
        bucket(q)

    pl.semaphore_wait(barrier, leaves - 1 + SIZE_X)

    for q in range(2):

        def send(k, carry):
            to = peer(k)
            pltpu.make_async_remote_copy(
                packed.at[q, to], got.at[q, me], a_send.at[q], a_recv.at[q],
                device_id={"leaf": to}, device_id_type=MESH,
            ).start()
            pltpu.make_async_remote_copy(
                packed_w.at[q, to], got_w.at[q, me], w_send.at[q], w_recv.at[q],
                device_id={"leaf": to}, device_id_type=MESH,
            ).start()
            return carry

        lax.fori_loop(1, leaves, send, 0)
    keep = []
    for q in range(2):
        keep.append(pltpu.make_async_copy(packed.at[q, me], got.at[q, me], own_sem.at[0, q]))
        keep.append(pltpu.make_async_copy(packed_w.at[q, me], got_w.at[q, me], own_sem.at[1, q]))
    for copy in keep:
        copy.start()

    children, rows_leaf = leaf_rows.shape[1], leaf_rows.shape[2]
    eye = lax.broadcasted_iota(jnp.int32, (rows_leaf, rows_leaf), 0) == lax.broadcasted_iota(
        jnp.int32, (rows_leaf, rows_leaf), 1
    )
    for q in range(2):
        scaled = []
        for b in range(children):
            w = leaf_weight[q, b : b + 1, :].astype(F32)
            w = jnp.sum(jnp.where(eye, w, 0.0), axis=1, keepdims=True)
            alive = (b < branching[q]).astype(F32)
            scaled.append((leaf_rows[q, b].astype(F32) * (w * alive)).astype(BF16))
        both = jnp.concatenate(scaled, axis=0)
        total = outer_sum(both, leaf_rows[q].reshape(children * rows_leaf, state))
        part[q] = total.reshape(SIZE_YH, SIZE_X, block, state)

    def rows_of(q):
        for copy in keep[2 * q : 2 * q + 2]:
            copy.wait()
        some = pl.ds(0, leaves - 1)
        pltpu.make_async_remote_copy(
            packed.at[q, some], got.at[q, some], a_send.at[q], a_recv.at[q],
            device_id={"leaf": partner}, device_id_type=MESH,
        ).wait_recv()
        pltpu.make_async_remote_copy(
            packed_w.at[q, some], got_w.at[q, some], w_send.at[q], w_recv.at[q],
            device_id={"leaf": partner}, device_id_type=MESH,
        ).wait_recv()
        total = leaves * GROUP
        r = lax.broadcasted_iota(jnp.int32, (total, lanes), 0) % GROUP
        tiles = [got[q, :, c].astype(F32).reshape(total, lanes) for c in range(3)]
        tail = jnp.zeros((total, lanes), F32)
        for c in range(3):
            moved = pltpu.roll(tiles[c], total - (CAP - 2 * c), 0)
            tail = jnp.where((r // 2) == c, moved, tail)
        r3 = lax.broadcasted_iota(jnp.int32, (leaves, GROUP, lanes), 1)
        l3 = lax.broadcasted_iota(jnp.int32, (leaves, GROUP, lanes), 2)
        w = jnp.where((r3 == l3) & (r3 < CAP), got_w[q], 0.0)
        w = jnp.sum(w, axis=2, keepdims=True).reshape(total, 1)
        plain = [t.astype(BF16) for t in tiles + [tail]]
        scaled = [(t * w).astype(BF16) for t in tiles + [tail]]
        return jnp.concatenate(scaled, axis=1), jnp.concatenate(plain, axis=1)

    def x_copy(q, dx):
        to = (at_x + dx) % SIZE_X
        return pltpu.make_async_remote_copy(
            xs.at[q, :, to], xr.at[q, dx - 1], x_send.at[q, dx - 1], x_recv.at[q, dx - 1],
            device_id={"blk": x_peer(dx)}, device_id_type=MESH,
        )

    def y_copy(q):
        return pltpu.make_async_remote_copy(
            ys.at[q], yr.at[q], y_send.at[q], y_recv.at[q],
            device_id={"blk": yh_peer}, device_id_type=MESH,
        )

    def p_copy(q):
        return pltpu.make_async_remote_copy(
            schur_out.at[q], pr.at[q], p_send.at[q], p_recv.at[q],
            device_id={"leaf": partner}, device_id_type=MESH,
        )

    def reduce_x(q):
        scaled, plain = rows_of(q)
        total = part[q] + outer_sum(scaled, plain).reshape(SIZE_YH, SIZE_X, block, state)
        part[q] = total
        xs[q] = total.astype(WIRE)
        for dx in (2, 1, 3):
            x_copy(q, dx).start()

    def reduce_y(q):
        for dx in (1, 3, 2):
            x_copy(q, dx).wait_recv()
        away = part[q, 1 - at_yh, at_x]
        for dx in range(SIZE_X - 1):
            away = away + xr[q, dx, 1 - at_yh].astype(F32)
        ys[q] = away.astype(WIRE)
        y_copy(q).start()
        mine = part[q, at_yh, at_x]
        for dx in range(SIZE_X - 1):
            mine = mine + xr[q, dx, at_yh].astype(F32)
        half[q] = mine + node_block[:, q, :].astype(F32)

    def finish(q):
        y_copy(q).wait_recv()
        schur_out[q] = half[q] + yr[q].astype(F32)
        p_copy(q).start()

    reduce_x(0)
    reduce_y(0)
    reduce_x(1)
    reduce_y(1)
    finish(0)
    finish(1)
    for q in range(2):
        p_copy(q).wait_recv()
    for q in range(2):
        choice = jnp.full((block, state), sibling[0, q], jnp.int32)
        merged_out[q] = schur_out[q] + jnp.where(choice == 0, pr[0], pr[1])

    some = pl.ds(0, leaves - 1)
    for q in range(2):
        pltpu.make_async_remote_copy(
            packed.at[q, some], got.at[q, some], a_send.at[q], a_recv.at[q],
            device_id={"leaf": partner}, device_id_type=MESH,
        ).wait_send()
        pltpu.make_async_remote_copy(
            packed_w.at[q, some], got_w.at[q, some], w_send.at[q], w_recv.at[q],
            device_id={"leaf": partner}, device_id_type=MESH,
        ).wait_send()
        for dx in range(1, SIZE_X):
            x_copy(q, dx).wait_send()
        y_copy(q).wait_send()
        p_copy(q).wait_send()


def shards(leaf_rows, leaf_weight, branching, sibling, node_block, na_rows, na_weight, na_route):
    leaves = ROWS_Y * ROWS_Z * CORES
    count, state = na_rows.shape
    block = state // (SIZE_X * SIZE_YH)
    vmem = pl.BlockSpec(memory_space=pltpu.VMEM)
    smem = pl.BlockSpec(memory_space=pltpu.SMEM)
    dma = pltpu.SemaphoreType.DMA
    schur, merged = pl.pallas_call(
        kernel,
        out_shape=[jax.ShapeDtypeStruct((2, block, state), F32)] * 2,
        in_specs=[smem, smem] + [vmem] * 6,
        out_specs=[vmem, vmem],
        scratch_shapes=[
            pltpu.VMEM((2, leaves, 3, GROUP, 128), BF16),
            pltpu.VMEM((2, leaves, 1, 128), F32),
            pltpu.VMEM((2, leaves, 3, GROUP, 128), BF16),
            pltpu.VMEM((2, leaves, 1, 128), F32),
            pltpu.VMEM((2, SIZE_YH, SIZE_X, block, state), F32),
            pltpu.VMEM((2, block, state), F32),
            pltpu.VMEM((2, SIZE_YH, SIZE_X, block, state), WIRE),
            pltpu.VMEM((2, SIZE_X - 1, SIZE_YH, block, state), WIRE),
            pltpu.VMEM((2, block, state), WIRE),
            pltpu.VMEM((2, block, state), WIRE),
            pltpu.VMEM((2, block, state), F32),
            dma((2,)),
            dma((2,)),
            dma((2,)),
            dma((2,)),
            dma((2, SIZE_X - 1)),
            dma((2, SIZE_X - 1)),
            dma((2,)),
            dma((2,)),
            dma((2,)),
            dma((2,)),
            dma((2, 2)),
        ],
        compiler_params=pltpu.CompilerParams(
            collective_id=0, has_side_effects=True, vmem_limit_bytes=60 << 20
        ),
        name="schur_pass",
    )(
        branching,
        sibling,
        leaf_rows,
        leaf_weight,
        node_block,
        na_rows,
        na_weight.reshape(1, count),
        na_route.reshape(1, count),
    )
    return jnp.transpose(schur, (1, 0, 2)), jnp.transpose(merged, (1, 0, 2))


def solution(mesh):
    return jax.shard_map(
        shards,
        mesh=mesh,
        in_specs=(
            P("leaf", None, "blk", None),
            P("leaf", None, "blk"),
            P("leaf"),
            P("leaf", None),
            P("blk", "leaf", None),
            P(("leaf", "blk"), None),
            P(("leaf", "blk")),
            P(("leaf", "blk"), None),
        ),
        out_specs=(P("blk", "leaf", None), P("blk", "leaf", None)),
        check_vma=False,
    )
```

time: 233 us -> 80.3 us (0.34)
  waiting for transfers between devices: 124 us -> 0 us
  Pallas kernels: 0 us -> 75.4 us
  local copies, waits for them, and re-layouts: 56.1 us -> 4.06 us
  starting transfers between devices: 27.4 us -> 0 us
  between operations: 14.2 us -> 0.66 us
  other arithmetic: 6.58 us -> 0 us
  matrix products: 4.41 us -> 0 us
    reduce_scatter x1 -> x0, waiting for transfers between devices: 94 us -> none  [shards(): lax.psum_scatter(jnp.einsum('nbks,nbkt->snt', sliced, leaf_rows, preferre...]
    pallas_call x0 -> x1, Pallas kernels: none -> 75.4 us  [shards(): pl.pallas_call(kernel, out_shape=[jax.ShapeDtypeStruct((2, block, state),...]
    gather x12 -> x0, local copies, waits for them, and re-layouts: 42.1 us -> none  [the longest x10 34.9 us: bucket_rows(): first = jnp.searchsorted(sorted_route, sorted_route, side='left')]
    all_to_all x2 -> x0, waiting for transfers between devices: 29.4 us -> none  [the longest x1 26.1 us: shards(): lax.all_to_all(filled.reshape(leaf_count, node_dev * capacity, state), 'l...]
    all_to_all x2 -> x0, starting transfers between devices: 23 us -> none  [the longest x1 15.4 us: shards(): lax.all_to_all(fill_weights.reshape(leaf_count, node_dev * capacity), 'le...]
    scatter x2 -> x0, local copies, waits for them, and re-layouts: 8.71 us -> none  [the longest x1 4.94 us: bucket_rows(): jnp.zeros((total_nodes * capacity, width), rows.dtype).at[slot]]
    sort x1 -> x0, other arithmetic: 4.5 us -> none  [bucket_rows(): order = jnp.argsort(route, stable=True)]
    ppermute x1 -> x0, starting transfers between devices: 4.41 us -> none  [from_partner(): lax.ppermute(shard, axis, [(i, i ^ 1 << apart) for i in range(lax.axis_si...]
  transfers between devices with their start and end apart: 4 -> 0, of which waited for: 4 -> 0; matrix products, arithmetic and copies ran while one was open for 4% -> 0% of each run, Pallas kernels for 0% -> 0%
where the time goes in v1:
time: 80.3 us; the launch traced here: 80.1 us
  Pallas kernels  75.4 us (94%)
  local copies, waits for them, and re-layouts  4.06 us (5%)
    pallas_call x1, Pallas kernels, shards(): pl.pallas_call(kernel, out_shape=[jax.ShapeDtypeStruct((2, block, state),...  75.4 us
    unnamed x6, local copies, waits for them, and re-layouts  3.48 us

profile of v1, /device:TPU:1, one launch (start us, length us, event | category | flops | bytes accessed | tf_op | source)
XLA Modules:
  0.0 80.1 jit_solution(13896447336527929226)
XLA Ops:
  0.6 0.0 copy-start.1
  0.6 0.7 copy-done.1
  1.3 0.6 reshape.10.na_weight
  1.9 75.4 %schur_pass.1 = (f32[2,64,512]{2,1,0:T(8,128)}, f32[2,64,512]{2,1,0:T(8,128)}) custom-call(s32[2]{0:T(128)} %branching.1, s32[1,2]{1,0:T(1,128)} %sibling.1, bf16[2,8,64,512]{3,2,1,0:T(8,128)(2,1)} %leaf_rows.1, bf16[2,8,64]{2,1,0:T(8,128)(2,1)} %leaf_weight.1, bf16[64,2,512]{2,1,0:T(2,128)(2,1)} %node_block.1, bf16[512,512]{1,0:T(8,128)(2,1)} %na_rows.1, ...), custom_call_target="tpu_custom_call" | custom-call | tf_op jit(solution)/shard_map/schur_pass/pallas_call | solution.py:285
  77.3 0.0 copy-start
  77.3 1.9 %copy.10 = f32[64,2,512]{2,1,0:T(2,128)} copy(f32[64,2,512]{2,0,1:T(8,128)} %bitcast.4) | data formatting | bytes 524288
  79.2 0.0 copy-done
  79.2 0.9 %copy.11 = f32[64,2,512]{2,1,0:T(2,128)} copy(f32[64,2,512]{2,0,1:T(8,128)S(1)} %bitcast.3) | data formatting | bytes 524288
Async XLA Ops:
  0.6 0.7 copy-start.1
  77.3 1.9 %copy-start = (f32[2,64,512]{2,1,0:T(8,128)S(1)}, f32[2,64,512]{2,1,0:T(8,128)}, u32[]{:S(2)}) copy-start(f32[2,64,512]{2,1,0:T(8,128)} %get-tuple-element.5) | copy-start | bytes 786436

commit v2 on v1

--- a/solution.py
+++ b/solution.py
@@ -10,11 +10,36 @@
 MESH = pl.DeviceIdType.MESH
 F32 = jnp.float32
 BF16 = jnp.bfloat16
-WIRE = jnp.float32
+WIRE = jnp.int16
+TOP = 32000.0
 ROWS_Y, ROWS_Z, CORES = 4, 8, 2
 SIZE_X, SIZE_YH = 4, 2
 CAP = 6
 GROUP = 8
+
+
+def column_of(row, height):
+    eye = lax.broadcasted_iota(jnp.int32, (height, row.shape[1]), 0) == lax.broadcasted_iota(
+        jnp.int32, (height, row.shape[1]), 1
+    )
+    return jnp.sum(jnp.where(eye, row, 0.0), axis=1, keepdims=True)
+
+
+def row_of(column):
+    eye = lax.broadcasted_iota(jnp.int32, (column.shape[0], 128), 0) == lax.broadcasted_iota(
+        jnp.int32, (column.shape[0], 128), 1
+    )
+    return jnp.sum(jnp.where(eye, column, 0.0), axis=0, keepdims=True)
+
+
+def to_wire(values):
+    peak = jnp.max(jnp.abs(values), axis=1, keepdims=True)
+    peak = jnp.maximum(peak, 1e-30)
+    return jnp.round(values * (TOP / peak)).astype(jnp.int32).astype(WIRE), peak * (1.0 / TOP)
+
+
+def from_wire(values, unit_row):
+    return values.astype(jnp.int32).astype(F32) * column_of(unit_row, values.shape[0])
 
 
 def outer_sum(scaled, plain):
@@ -41,9 +66,13 @@
     part,
     half,
     xs,
+    xs_unit,
     xr,
+    xr_unit,
     ys,
+    ys_unit,
     yr,
+    yr_unit,
     pr,
     a_send,
     a_recv,
@@ -51,8 +80,12 @@
     w_recv,
     x_send,
     x_recv,
+    xu_send,
+    xu_recv,
     y_send,
     y_recv,
+    yu_send,
+    yu_recv,
     p_send,
     p_recv,
     own_sem,
@@ -67,12 +100,11 @@
     lanes = 128
     block = state // (SIZE_X * SIZE_YH)
 
-    def peer(k):
-        mixed = (k * 27) % leaves
-        to_core = (core + mixed % CORES) % CORES
-        to_z = (at_z + (mixed // CORES) % ROWS_Z) % ROWS_Z
-        to_y = (at_y + mixed // (CORES * ROWS_Z)) % ROWS_Y
-        return (to_y * ROWS_Z + to_z) * CORES + to_core
+    chips = ROWS_Y * ROWS_Z
+
+    def chip_at(j):
+        far = (j * 13) % chips
+        return ((at_y + far // ROWS_Z) % ROWS_Y) * ROWS_Z + (at_z + far) % ROWS_Z
 
     def x_peer(dx):
         return at_yh * SIZE_X + (at_x + dx) % SIZE_X
@@ -82,11 +114,14 @@
 
     barrier = pltpu.get_barrier_semaphore()
 
-    def greet(k, carry):
-        pl.semaphore_signal(barrier, inc=1, device_id={"leaf": peer(k)}, device_id_type=MESH)
+    def greet(j, carry):
+        to = chip_at(j) * CORES
+        for c in range(CORES):
+            pl.semaphore_signal(barrier, inc=1, device_id={"leaf": to + c}, device_id_type=MESH)
         return carry
 
-    lax.fori_loop(1, leaves, greet, 0)
+    lax.fori_loop(1, chips, greet, 0)
+    pl.semaphore_signal(barrier, inc=1, device_id={"leaf": partner}, device_id_type=MESH)
     for dx in range(1, SIZE_X):
         pl.semaphore_signal(barrier, inc=1, device_id={"blk": x_peer(dx)}, device_id_type=MESH)
     pl.semaphore_signal(barrier, inc=1, device_id={"blk": yh_peer}, device_id_type=MESH)
@@ -105,7 +140,7 @@
         same = (column == route_f) & (earlier < later)
         place = place + jnp.sum(jnp.where(same, 1.0, 0.0), axis=0, keepdims=True)
     slot = (route % 2) * (leaves * GROUP) + (route // 2) * GROUP + place.astype(jnp.int32)
-    weight = na_weight[...].astype(F32)
+    weight = na_weight[...].astype(F32).reshape(1, count)
 
     span = 128
     spans = leaves * GROUP // span
@@ -127,8 +162,9 @@
                 tile = jnp.where(rank < CAP, filled[:, c * lanes : (c + 1) * lanes], moved)
                 packed[q, at, c] = tile.reshape(subs, GROUP, lanes).astype(BF16)
             slot_w = jnp.sum(jnp.where(hit, weight, 0.0), axis=1, keepdims=True)
-            spread = jnp.where(rank == lane, slot_w, 0.0).reshape(subs, GROUP, lanes)
-            packed_w[q, at] = jnp.sum(spread, axis=1, keepdims=True)
+            spread = jnp.where(rank + q * GROUP == lane, slot_w, 0.0).reshape(subs, GROUP, lanes)
+            spread = jnp.sum(spread, axis=1, keepdims=True)
+            packed_w[at] = spread if q == 0 else packed_w[at] + spread
             return carry
 
         lax.fori_loop(0, spans, one, 0)
@@ -138,25 +174,51 @@
 
     pl.semaphore_wait(barrier, leaves - 1 + SIZE_X)
 
-    for q in range(2):
-
-        def send(k, carry):
-            to = peer(k)
-            pltpu.make_async_remote_copy(
-                packed.at[q, to], got.at[q, me], a_send.at[q], a_recv.at[q],
-                device_id={"leaf": to}, device_id_type=MESH,
-            ).start()
-            pltpu.make_async_remote_copy(
-                packed_w.at[q, to], got_w.at[q, me], w_send.at[q], w_recv.at[q],
-                device_id={"leaf": to}, device_id_type=MESH,
-            ).start()
-            return carry
-
-        lax.fori_loop(1, leaves, send, 0)
+    def w_copy(to):
+        return pltpu.make_async_remote_copy(
+            packed_w.at[to], got_w.at[me], w_send, w_recv,
+            device_id={"leaf": to}, device_id_type=MESH,
+        )
+
+    def a_copy(q, to):
+        return pltpu.make_async_remote_copy(
+            packed.at[q, to], got.at[q, me], a_send.at[q], a_recv.at[q],
+            device_id={"leaf": to}, device_id_type=MESH,
+        )
+
+    w_copy(partner).start()
+    for q in range(2):
+        a_copy(q, partner).start()
+    for q in range(2):
+        for c in range(CORES):
+
+            def send(j, carry):
+                to = chip_at(j) * CORES + c
+                if q == 0:
+                    w_copy(to).start()
+                a_copy(q, to).start()
+                return carry
+
+            lax.fori_loop(1, chips, send, 0)
+
+    some = pl.ds(0, leaves - 1)
+
+    def all_rows(q):
+        return pltpu.make_async_remote_copy(
+            packed.at[q, some], got.at[q, some], a_send.at[q], a_recv.at[q],
+            device_id={"leaf": partner}, device_id_type=MESH,
+        )
+
+    def all_weights():
+        return pltpu.make_async_remote_copy(
+            packed_w.at[some], got_w.at[some], w_send, w_recv,
+            device_id={"leaf": partner}, device_id_type=MESH,
+        )
+
     keep = []
     for q in range(2):
         keep.append(pltpu.make_async_copy(packed.at[q, me], got.at[q, me], own_sem.at[0, q]))
-        keep.append(pltpu.make_async_copy(packed_w.at[q, me], got_w.at[q, me], own_sem.at[1, q]))
+    keep.append(pltpu.make_async_copy(packed_w.at[me], got_w.at[me], own_sem.at[1, 0]))
     for copy in keep:
         copy.start()
 
@@ -176,17 +238,11 @@
         part[q] = total.reshape(SIZE_YH, SIZE_X, block, state)
 
     def rows_of(q):
-        for copy in keep[2 * q : 2 * q + 2]:
-            copy.wait()
-        some = pl.ds(0, leaves - 1)
-        pltpu.make_async_remote_copy(
-            packed.at[q, some], got.at[q, some], a_send.at[q], a_recv.at[q],
-            device_id={"leaf": partner}, device_id_type=MESH,
-        ).wait_recv()
-        pltpu.make_async_remote_copy(
-            packed_w.at[q, some], got_w.at[q, some], w_send.at[q], w_recv.at[q],
-            device_id={"leaf": partner}, device_id_type=MESH,
-        ).wait_recv()
+        keep[q].wait()
+        if q == 0:
+            keep[2].wait()
+            all_weights().wait_recv()
+        all_rows(q).wait_recv()
         total = leaves * GROUP
         r = lax.broadcasted_iota(jnp.int32, (total, lanes), 0) % GROUP
         tiles = [got[q, :, c].astype(F32).reshape(total, lanes) for c in range(3)]
@@ -196,23 +252,36 @@
             tail = jnp.where((r // 2) == c, moved, tail)
         r3 = lax.broadcasted_iota(jnp.int32, (leaves, GROUP, lanes), 1)
         l3 = lax.broadcasted_iota(jnp.int32, (leaves, GROUP, lanes), 2)
-        w = jnp.where((r3 == l3) & (r3 < CAP), got_w[q], 0.0)
+        w = jnp.where((r3 + q * GROUP == l3) & (r3 < CAP), got_w[...], 0.0)
         w = jnp.sum(w, axis=2, keepdims=True).reshape(total, 1)
         plain = [t.astype(BF16) for t in tiles + [tail]]
         scaled = [(t * w).astype(BF16) for t in tiles + [tail]]
         return jnp.concatenate(scaled, axis=1), jnp.concatenate(plain, axis=1)
 
-    def x_copy(q, dx):
+    def x_copies(q, dx):
         to = (at_x + dx) % SIZE_X
-        return pltpu.make_async_remote_copy(
-            xs.at[q, :, to], xr.at[q, dx - 1], x_send.at[q, dx - 1], x_recv.at[q, dx - 1],
-            device_id={"blk": x_peer(dx)}, device_id_type=MESH,
-        )
-
-    def y_copy(q):
-        return pltpu.make_async_remote_copy(
-            ys.at[q], yr.at[q], y_send.at[q], y_recv.at[q],
-            device_id={"blk": yh_peer}, device_id_type=MESH,
+        ends = {"device_id": {"blk": x_peer(dx)}, "device_id_type": MESH}
+        i = dx - 1
+        unit = pltpu.make_async_remote_copy(
+            xs_unit.at[q, :, to], xr_unit.at[q, i], xu_send.at[q, i], xu_recv.at[q, i], **ends
+        )
+        away, near = (
+            pltpu.make_async_remote_copy(
+                xs.at[q, yh, to], xr.at[q, i, yh], x_send.at[q, i, k], x_recv.at[q, i, k], **ends
+            )
+            for k, yh in enumerate((1 - at_yh, at_yh))
+        )
+        return unit, away, near
+
+    def y_copies(q):
+        ends = {"device_id": {"blk": yh_peer}, "device_id_type": MESH}
+        return (
+            pltpu.make_async_remote_copy(
+                ys_unit.at[q], yr_unit.at[q], yu_send.at[q], yu_recv.at[q], **ends
+            ),
+            pltpu.make_async_remote_copy(
+                ys.at[q], yr.at[q], y_send.at[q], y_recv.at[q], **ends
+            ),
         )
 
     def p_copy(q):
@@ -225,26 +294,38 @@
         scaled, plain = rows_of(q)
         total = part[q] + outer_sum(scaled, plain).reshape(SIZE_YH, SIZE_X, block, state)
         part[q] = total
-        xs[q] = total.astype(WIRE)
-        for dx in (2, 1, 3):
-            x_copy(q, dx).start()
+        for yh in range(SIZE_YH):
+            for x in range(SIZE_X):
+                xs[q, yh, x], unit = to_wire(total[yh, x])
+                xs_unit[q, yh, x] = row_of(unit)
+        order = [x_copies(q, dx) for dx in (2, 1, 3)]
+        for k in range(3):
+            for copies in order:
+                copies[k].start()
+
+    def sum_x(q, yh):
+        total = part[q, yh, at_x]
+        for i in range(SIZE_X - 1):
+            total = total + from_wire(xr[q, i, yh], xr_unit[q, i, yh])
+        return total
 
     def reduce_y(q):
-        for dx in (1, 3, 2):
-            x_copy(q, dx).wait_recv()
-        away = part[q, 1 - at_yh, at_x]
-        for dx in range(SIZE_X - 1):
-            away = away + xr[q, dx, 1 - at_yh].astype(F32)
-        ys[q] = away.astype(WIRE)
-        y_copy(q).start()
-        mine = part[q, at_yh, at_x]
-        for dx in range(SIZE_X - 1):
-            mine = mine + xr[q, dx, at_yh].astype(F32)
-        half[q] = mine + node_block[:, q, :].astype(F32)
+        order = [x_copies(q, dx) for dx in (1, 3, 2)]
+        for k in range(2):
+            for copies in order:
+                copies[k].wait_recv()
+        ys[q], unit = to_wire(sum_x(q, 1 - at_yh))
+        ys_unit[q] = row_of(unit)
+        for copy in y_copies(q):
+            copy.start()
+        for copies in order:
+            copies[2].wait_recv()
+        half[q] = sum_x(q, at_yh) + node_block[:, q, :].astype(F32)
 
     def finish(q):
-        y_copy(q).wait_recv()
-        schur_out[q] = half[q] + yr[q].astype(F32)
+        for copy in y_copies(q):
+            copy.wait_recv()
+        schur_out[q] = half[q] + from_wire(yr[q], yr_unit[q])
         p_copy(q).start()
 
     reduce_x(0)
@@ -259,20 +340,21 @@
         choice = jnp.full((block, state), sibling[0, q], jnp.int32)
         merged_out[q] = schur_out[q] + jnp.where(choice == 0, pr[0], pr[1])
 
-    some = pl.ds(0, leaves - 1)
-    for q in range(2):
-        pltpu.make_async_remote_copy(
-            packed.at[q, some], got.at[q, some], a_send.at[q], a_recv.at[q],
-            device_id={"leaf": partner}, device_id_type=MESH,
-        ).wait_send()
-        pltpu.make_async_remote_copy(
-            packed_w.at[q, some], got_w.at[q, some], w_send.at[q], w_recv.at[q],
-            device_id={"leaf": partner}, device_id_type=MESH,
-        ).wait_send()
+    all_weights().wait_send()
+    for q in range(2):
+        all_rows(q).wait_send()
         for dx in range(1, SIZE_X):
-            x_copy(q, dx).wait_send()
-        y_copy(q).wait_send()
+            for copy in x_copies(q, dx):
+                copy.wait_send()
+        for copy in y_copies(q):
+            copy.wait_send()
         p_copy(q).wait_send()
+
+
+def arrange(schur, merged, schur_out, merged_out):
+    for q in range(2):
+        schur_out[:, q, :] = schur[q]
+        merged_out[:, q, :] = merged[q]
 
 
 def shards(leaf_rows, leaf_weight, branching, sibling, node_block, na_rows, na_weight, na_route):
@@ -289,22 +371,30 @@
         out_specs=[vmem, vmem],
         scratch_shapes=[
             pltpu.VMEM((2, leaves, 3, GROUP, 128), BF16),
-            pltpu.VMEM((2, leaves, 1, 128), F32),
+            pltpu.VMEM((leaves, 1, 128), F32),
             pltpu.VMEM((2, leaves, 3, GROUP, 128), BF16),
-            pltpu.VMEM((2, leaves, 1, 128), F32),
+            pltpu.VMEM((leaves, 1, 128), F32),
             pltpu.VMEM((2, SIZE_YH, SIZE_X, block, state), F32),
             pltpu.VMEM((2, block, state), F32),
             pltpu.VMEM((2, SIZE_YH, SIZE_X, block, state), WIRE),
+            pltpu.VMEM((2, SIZE_YH, SIZE_X, 1, 128), F32),
             pltpu.VMEM((2, SIZE_X - 1, SIZE_YH, block, state), WIRE),
+            pltpu.VMEM((2, SIZE_X - 1, SIZE_YH, 1, 128), F32),
             pltpu.VMEM((2, block, state), WIRE),
+            pltpu.VMEM((2, 1, 128), F32),
             pltpu.VMEM((2, block, state), WIRE),
+            pltpu.VMEM((2, 1, 128), F32),
             pltpu.VMEM((2, block, state), F32),
             dma((2,)),
             dma((2,)),
-            dma((2,)),
-            dma((2,)),
+            dma(()),
+            dma(()),
+            dma((2, SIZE_X - 1, 2)),
+            dma((2, SIZE_X - 1, 2)),
             dma((2, SIZE_X - 1)),
             dma((2, SIZE_X - 1)),
+            dma((2,)),
+            dma((2,)),
             dma((2,)),
             dma((2,)),
             dma((2,)),
@@ -322,10 +412,16 @@
         leaf_weight,
         node_block,
         na_rows,
-        na_weight.reshape(1, count),
+        na_weight,
         na_route.reshape(1, count),
     )
-    return jnp.transpose(schur, (1, 0, 2)), jnp.transpose(merged, (1, 0, 2))
+    return pl.pallas_call(
+        arrange,
+        out_shape=[jax.ShapeDtypeStruct((block, 2, state), F32)] * 2,
+        in_specs=[vmem, vmem],
+        out_specs=[vmem, vmem],
+        name="arrange",
+    )(schur, merged)
 
 
 def solution(mesh):

time: 80.3 us -> 57.6 us (0.72)
  Pallas kernels: 75.4 us -> 56.8 us
  local copies, waits for them, and re-layouts: 4.06 us -> 0 us
    pallas_call x1, Pallas kernels: 75.4 us -> 54.9 us  [shards(): pl.pallas_call(kernel, out_shape=[jax.ShapeDtypeStruct((2, block, state),...]
    unnamed x6 -> x0, local copies, waits for them, and re-layouts: 3.48 us -> none
    pallas_call x0 -> x1, Pallas kernels: none -> 1.9 us  [shards(): pl.pallas_call(arrange, out_shape=[jax.ShapeDtypeStruct((block, 2, state)...]
where the time goes in v2:
time: 57.6 us; the launch traced here: 57.4 us
  Pallas kernels  56.8 us (99%)
  between operations  0.64 us (1%)
    pallas_call x1, Pallas kernels, shards(): pl.pallas_call(kernel, out_shape=[jax.ShapeDtypeStruct((2, block, state),...  54.9 us
    pallas_call x1, Pallas kernels, shards(): pl.pallas_call(arrange, out_shape=[jax.ShapeDtypeStruct((block, 2, state)...  1.9 us

profile of v2, /device:TPU:1, one launch (start us, length us, event | category | flops | bytes accessed | tf_op | source)
XLA Modules:
  0.0 57.4 jit_solution(2647531852823212267)
XLA Ops:
  0.6 54.9 %schur_pass.1 = (f32[2,64,512]{2,1,0:T(8,128)}, f32[2,64,512]{2,1,0:T(8,128)}) custom-call(s32[2]{0:T(128)} %branching.1, s32[1,2]{1,0:T(1,128)} %sibling.1, bf16[2,8,64,512]{3,2,1,0:T(8,128)(2,1)} %leaf_rows.1, bf16[2,8,64]{2,1,0:T(8,128)(2,1)} %leaf_weight.1, bf16[64,2,512]{2,1,0:T(2,128)(2,1)} %node_block.1, bf16[512,512]{1,0:T(8,128)(2,1)} %na_rows.1, ...), custom_call_target="tpu_custom_call" | custom-call | tf_op jit(solution)/shard_map/schur_pass/pallas_call | solution.py:367
  55.5 1.9 %arrange.1 = (f32[64,2,512]{2,1,0:T(2,128)}, f32[64,2,512]{2,1,0:T(2,128)}) custom-call(f32[2,64,512]{2,1,0:T(8,128)} %get-tuple-element.4.schur, f32[2,64,512]{2,1,0:T(8,128)} %get-tuple-element.5.merged), custom_call_target="tpu_custom_call" | custom-call | tf_op jit(solution)/shard_map/arrange/pallas_call | solution.py:418

commit v3 on v2

--- a/solution.py
+++ b/solution.py
@@ -51,14 +51,17 @@
 def kernel(
     branching,
     sibling,
-    leaf_rows,
+    leaf_rows_in,
     leaf_weight,
-    node_block,
-    na_rows,
+    node_block_in,
+    na_rows_in,
     na_weight,
     na_route,
     schur_out,
     merged_out,
+    leaf_rows,
+    node_block,
+    na_rows,
     packed,
     packed_w,
     got,
@@ -89,6 +92,7 @@
     p_send,
     p_recv,
     own_sem,
+    in_sem,
 ):
     leaves = ROWS_Y * ROWS_Z * CORES
     me = lax.axis_index("leaf")
@@ -103,14 +107,24 @@
     chips = ROWS_Y * ROWS_Z
 
     def chip_at(j):
-        far = (j * 13) % chips
-        return ((at_y + far // ROWS_Z) % ROWS_Y) * ROWS_Z + (at_z + far) % ROWS_Z
+        a = j // ROWS_Y
+        dz = ROWS_Z // 2 + (a // 2 + a % 2) * (1 - 2 * (a % 2))
+        dy = ROWS_Y - 1 - j % ROWS_Y
+        return ((at_y + dy) % ROWS_Y) * ROWS_Z + (at_z + dz) % ROWS_Z
 
     def x_peer(dx):
         return at_yh * SIZE_X + (at_x + dx) % SIZE_X
 
     yh_peer = (1 - at_yh) * SIZE_X + at_x
     partner = (me // CORES) * CORES + (1 - core)
+
+    loads = [
+        pltpu.make_async_copy(na_rows_in, na_rows, in_sem.at[0]),
+        pltpu.make_async_copy(leaf_rows_in, leaf_rows, in_sem.at[1]),
+        pltpu.make_async_copy(node_block_in, node_block, in_sem.at[2]),
+    ]
+    for load in loads:
+        load.start()
 
     barrier = pltpu.get_barrier_semaphore()
 
@@ -120,7 +134,7 @@
             pl.semaphore_signal(barrier, inc=1, device_id={"leaf": to + c}, device_id_type=MESH)
         return carry
 
-    lax.fori_loop(1, chips, greet, 0)
+    lax.fori_loop(0, chips - 1, greet, 0)
     pl.semaphore_signal(barrier, inc=1, device_id={"leaf": partner}, device_id_type=MESH)
     for dx in range(1, SIZE_X):
         pl.semaphore_signal(barrier, inc=1, device_id={"blk": x_peer(dx)}, device_id_type=MESH)
@@ -169,6 +183,7 @@
 
         lax.fori_loop(0, spans, one, 0)
 
+    loads[0].wait()
     for q in range(2):
         bucket(q)
 
@@ -189,17 +204,16 @@
     w_copy(partner).start()
     for q in range(2):
         a_copy(q, partner).start()
-    for q in range(2):
-        for c in range(CORES):
-
-            def send(j, carry):
-                to = chip_at(j) * CORES + c
-                if q == 0:
-                    w_copy(to).start()
-                a_copy(q, to).start()
-                return carry
-
-            lax.fori_loop(1, chips, send, 0)
+    for q, c in ((0, 1), (0, 0), (1, 0), (1, 1)):
+
+        def send(j, carry):
+            to = chip_at(j) * CORES + c
+            if q == 0:
+                w_copy(to).start()
+            a_copy(q, to).start()
+            return carry
+
+        lax.fori_loop(0, chips - 1, send, 0)
 
     some = pl.ds(0, leaves - 1)
 
@@ -221,6 +235,9 @@
     keep.append(pltpu.make_async_copy(packed_w.at[me], got_w.at[me], own_sem.at[1, 0]))
     for copy in keep:
         copy.start()
+
+    for load in loads[1:]:
+        load.wait()
 
     children, rows_leaf = leaf_rows.shape[1], leaf_rows.shape[2]
     eye = lax.broadcasted_iota(jnp.int32, (rows_leaf, rows_leaf), 0) == lax.broadcasted_iota(
@@ -329,8 +346,8 @@
         p_copy(q).start()
 
     reduce_x(0)
+    reduce_x(1)
     reduce_y(0)
-    reduce_x(1)
     reduce_y(1)
     finish(0)
     finish(1)
@@ -363,13 +380,17 @@
     block = state // (SIZE_X * SIZE_YH)
     vmem = pl.BlockSpec(memory_space=pltpu.VMEM)
     smem = pl.BlockSpec(memory_space=pltpu.SMEM)
+    hbm = pl.BlockSpec(memory_space=pl.ANY)
     dma = pltpu.SemaphoreType.DMA
     schur, merged = pl.pallas_call(
         kernel,
-        out_shape=[jax.ShapeDtypeStruct((2, block, state), F32)] * 2,
-        in_specs=[smem, smem] + [vmem] * 6,
+        out_shape=[pltpu.VMEM((2, block, state), F32)] * 2,
+        in_specs=[smem, smem, hbm, vmem, hbm, hbm, vmem, vmem],
         out_specs=[vmem, vmem],
         scratch_shapes=[
+            pltpu.VMEM(leaf_rows.shape, BF16),
+            pltpu.VMEM(node_block.shape, BF16),
+            pltpu.VMEM(na_rows.shape, BF16),
             pltpu.VMEM((2, leaves, 3, GROUP, 128), BF16),
             pltpu.VMEM((leaves, 1, 128), F32),
             pltpu.VMEM((2, leaves, 3, GROUP, 128), BF16),
@@ -400,6 +421,7 @@
             dma((2,)),
             dma((2,)),
             dma((2, 2)),
+            dma((3,)),
         ],
         compiler_params=pltpu.CompilerParams(
             collective_id=0, has_side_effects=True, vmem_limit_bytes=60 << 20
@@ -421,7 +443,10 @@
         in_specs=[vmem, vmem],
         out_specs=[vmem, vmem],
         name="arrange",
-    )(schur, merged)
+    )(
+        pltpu.with_memory_space_constraint(schur, pltpu.VMEM),
+        pltpu.with_memory_space_constraint(merged, pltpu.VMEM),
+    )
 
 
 def solution(mesh):

time: 57.6 us -> 53.8 us (0.934)
  Pallas kernels: 56.8 us -> 53 us
    pallas_call x1, Pallas kernels: 54.9 us -> 52.1 us  [shards(): pl.pallas_call(kernel, out_shape=[pltpu.VMEM((2, block, state), F32)] * 2...]
    pallas_call x1, Pallas kernels: 1.9 us -> 0.87 us  [shards(): pl.pallas_call(arrange, out_shape=[jax.ShapeDtypeStruct((block, 2, state)...]
where the time goes in v3:
time: 53.8 us; the launch traced here: 53.6 us
  Pallas kernels  53 us (99%)
  between operations  0.64 us (1%)
    pallas_call x1, Pallas kernels, shards(): pl.pallas_call(kernel, out_shape=[pltpu.VMEM((2, block, state), F32)] * 2...  52.1 us

profile of v3, /device:TPU:1, one launch (start us, length us, event | category | flops | bytes accessed | tf_op | source)
XLA Modules:
  0.0 53.6 jit_solution(1812585581130757220)
XLA Ops:
  0.6 52.1 %schur_pass.1 = (f32[2,64,512]{2,1,0:T(8,128)S(1)}, f32[2,64,512]{2,1,0:T(8,128)S(1)}) custom-call(s32[2]{0:T(128)} %branching.1, s32[1,2]{1,0:T(1,128)} %sibling.1, bf16[2,8,64,512]{3,2,1,0:T(8,128)(2,1)} %leaf_rows_in.1, bf16[2,8,64]{2,1,0:T(8,128)(2,1)} %leaf_weight.1, bf16[64,2,512]{2,1,0:T(2,128)(2,1)} %node_block_in.1, bf16[512,512]{1,0:T(8,128)(2,1)} %na_rows_in.1, ...), custom_call_target="tpu_custom_call" | custom-call | tf_op jit(solution)/shard_map/schur_pass/pallas_call | solution.py:385
  52.8 0.9 %arrange.1 = (f32[64,2,512]{2,1,0:T(2,128)}, f32[64,2,512]{2,1,0:T(2,128)}) custom-call(f32[2,64,512]{2,1,0:T(8,128)S(1)} %get-tuple-element.4.schur, f32[2,64,512]{2,1,0:T(8,128)S(1)} %get-tuple-element.5.merged), custom_call_target="tpu_custom_call" | custom-call | tf_op jit(solution)/shard_map/arrange/pallas_call | solution.py:440

commit v4 on v3

--- a/solution.py
+++ b/solution.py
@@ -49,19 +49,24 @@
 
 
 def kernel(
+    branching_in,
+    sibling_in,
+    leaf_rows_in,
+    leaf_weight_in,
+    node_block_in,
+    na_rows_in,
+    na_weight_in,
+    na_route_in,
+    schur_out,
+    merged_out,
     branching,
     sibling,
-    leaf_rows_in,
+    leaf_rows,
     leaf_weight,
-    node_block_in,
-    na_rows_in,
+    node_block,
+    na_rows,
     na_weight,
     na_route,
-    schur_out,
-    merged_out,
-    leaf_rows,
-    node_block,
-    na_rows,
     packed,
     packed_w,
     got,
@@ -119,9 +124,19 @@
     partner = (me // CORES) * CORES + (1 - core)
 
     loads = [
-        pltpu.make_async_copy(na_rows_in, na_rows, in_sem.at[0]),
-        pltpu.make_async_copy(leaf_rows_in, leaf_rows, in_sem.at[1]),
-        pltpu.make_async_copy(node_block_in, node_block, in_sem.at[2]),
+        pltpu.make_async_copy(src, dst, in_sem.at[i])
+        for i, (src, dst) in enumerate(
+            (
+                (na_route_in, na_route),
+                (na_weight_in, na_weight),
+                (na_rows_in, na_rows),
+                (leaf_weight_in, leaf_weight),
+                (leaf_rows_in, leaf_rows),
+                (node_block_in, node_block),
+                (branching_in, branching),
+                (sibling_in, sibling),
+            )
+        )
     ]
     for load in loads:
         load.start()
@@ -139,6 +154,9 @@
     for dx in range(1, SIZE_X):
         pl.semaphore_signal(barrier, inc=1, device_id={"blk": x_peer(dx)}, device_id_type=MESH)
     pl.semaphore_signal(barrier, inc=1, device_id={"blk": yh_peer}, device_id_type=MESH)
+
+    for load in loads[:3]:
+        load.wait()
 
     route = na_route[...]
     route_f = route.astype(F32)
@@ -183,7 +201,6 @@
 
         lax.fori_loop(0, spans, one, 0)
 
-    loads[0].wait()
     for q in range(2):
         bucket(q)
 
@@ -204,7 +221,7 @@
     w_copy(partner).start()
     for q in range(2):
         a_copy(q, partner).start()
-    for q, c in ((0, 1), (0, 0), (1, 0), (1, 1)):
+    def send_unit(q, c):
 
         def send(j, carry):
             to = chip_at(j) * CORES + c
@@ -215,28 +232,9 @@
 
         lax.fori_loop(0, chips - 1, send, 0)
 
-    some = pl.ds(0, leaves - 1)
-
-    def all_rows(q):
-        return pltpu.make_async_remote_copy(
-            packed.at[q, some], got.at[q, some], a_send.at[q], a_recv.at[q],
-            device_id={"leaf": partner}, device_id_type=MESH,
-        )
-
-    def all_weights():
-        return pltpu.make_async_remote_copy(
-            packed_w.at[some], got_w.at[some], w_send, w_recv,
-            device_id={"leaf": partner}, device_id_type=MESH,
-        )
-
-    keep = []
-    for q in range(2):
-        keep.append(pltpu.make_async_copy(packed.at[q, me], got.at[q, me], own_sem.at[0, q]))
-    keep.append(pltpu.make_async_copy(packed_w.at[me], got_w.at[me], own_sem.at[1, 0]))
-    for copy in keep:
-        copy.start()
-
-    for load in loads[1:]:
+    for q, c in ((0, 1), (0, 0)):
+        send_unit(q, c)
+    for load in loads[3:]:
         load.wait()
 
     children, rows_leaf = leaf_rows.shape[1], leaf_rows.shape[2]
@@ -253,6 +251,29 @@
         both = jnp.concatenate(scaled, axis=0)
         total = outer_sum(both, leaf_rows[q].reshape(children * rows_leaf, state))
         part[q] = total.reshape(SIZE_YH, SIZE_X, block, state)
+
+    for q, c in ((1, 0), (1, 1)):
+        send_unit(q, c)
+    some = pl.ds(0, leaves - 1)
+
+    def all_rows(q):
+        return pltpu.make_async_remote_copy(
+            packed.at[q, some], got.at[q, some], a_send.at[q], a_recv.at[q],
+            device_id={"leaf": partner}, device_id_type=MESH,
+        )
+
+    def all_weights():
+        return pltpu.make_async_remote_copy(
+            packed_w.at[some], got_w.at[some], w_send, w_recv,
+            device_id={"leaf": partner}, device_id_type=MESH,
+        )
+
+    keep = []
+    for q in range(2):
+        keep.append(pltpu.make_async_copy(packed.at[q, me], got.at[q, me], own_sem.at[0, q]))
+    keep.append(pltpu.make_async_copy(packed_w.at[me], got_w.at[me], own_sem.at[1, 0]))
+    for copy in keep:
+        copy.start()
 
     def rows_of(q):
         keep[q].wait()
@@ -379,18 +400,22 @@
     count, state = na_rows.shape
     block = state // (SIZE_X * SIZE_YH)
     vmem = pl.BlockSpec(memory_space=pltpu.VMEM)
-    smem = pl.BlockSpec(memory_space=pltpu.SMEM)
     hbm = pl.BlockSpec(memory_space=pl.ANY)
     dma = pltpu.SemaphoreType.DMA
     schur, merged = pl.pallas_call(
         kernel,
         out_shape=[pltpu.VMEM((2, block, state), F32)] * 2,
-        in_specs=[smem, smem, hbm, vmem, hbm, hbm, vmem, vmem],
+        in_specs=[hbm] * 8,
         out_specs=[vmem, vmem],
         scratch_shapes=[
+            pltpu.SMEM(branching.shape, jnp.int32),
+            pltpu.SMEM(sibling.shape, jnp.int32),
             pltpu.VMEM(leaf_rows.shape, BF16),
+            pltpu.VMEM(leaf_weight.shape, BF16),
             pltpu.VMEM(node_block.shape, BF16),
             pltpu.VMEM(na_rows.shape, BF16),
+            pltpu.VMEM(na_weight.shape, BF16),
+            pltpu.VMEM((1, count), jnp.int32),
             pltpu.VMEM((2, leaves, 3, GROUP, 128), BF16),
             pltpu.VMEM((leaves, 1, 128), F32),
             pltpu.VMEM((2, leaves, 3, GROUP, 128), BF16),
@@ -421,7 +446,7 @@
             dma((2,)),
             dma((2,)),
             dma((2, 2)),
-            dma((3,)),
+            dma((8,)),
         ],
         compiler_params=pltpu.CompilerParams(
             collective_id=0, has_side_effects=True, vmem_limit_bytes=60 << 20

time: 53.8 us -> 53 us (0.985)
  Pallas kernels: 53 us -> 52.2 us
    pallas_call x1, Pallas kernels: 52.1 us -> 51.4 us  [shards(): pl.pallas_call(kernel, out_shape=[pltpu.VMEM((2, block, state), F32)] * 2...]
where the time goes in v4:
time: 53 us; the launch traced here: 52.9 us
  Pallas kernels  52.2 us (98%)
  between operations  0.64 us (1%)
    pallas_call x1, Pallas kernels, shards(): pl.pallas_call(kernel, out_shape=[pltpu.VMEM((2, block, state), F32)] * 2...  51.4 us

profile of v4, /device:TPU:1, one launch (start us, length us, event | category | flops | bytes accessed | tf_op | source)
XLA Modules:
  0.0 52.9 jit_solution(13224812508796505644)
XLA Ops:
  0.6 51.4 %schur_pass.1 = (f32[2,64,512]{2,1,0:T(8,128)S(1)}, f32[2,64,512]{2,1,0:T(8,128)S(1)}) custom-call(s32[2]{0:T(128)} %branching_in.1, s32[1,2]{1,0:T(1,128)} %sibling_in.1, bf16[2,8,64,512]{3,2,1,0:T(8,128)(2,1)} %leaf_rows_in.1, bf16[2,8,64]{2,1,0:T(8,128)(2,1)} %leaf_weight_in.1, bf16[64,2,512]{2,1,0:T(2,128)(2,1)} %node_block_in.1, ...), custom_call_target="tpu_custom_call" | custom-call | tf_op jit(solution)/shard_map/schur_pass/pallas_call | solution.py:405
  52.0 0.9 %arrange.1 = (f32[64,2,512]{2,1,0:T(2,128)}, f32[64,2,512]{2,1,0:T(2,128)}) custom-call(f32[2,64,512]{2,1,0:T(8,128)S(1)} %get-tuple-element.4.schur, f32[2,64,512]{2,1,0:T(8,128)S(1)} %get-tuple-element.5.merged), custom_call_target="tpu_custom_call" | custom-call | tf_op jit(solution)/shard_map/arrange/pallas_call | solution.py:465

commit v5 on v4

--- a/solution.py
+++ b/solution.py
@@ -57,8 +57,8 @@
     na_rows_in,
     na_weight_in,
     na_route_in,
-    schur_out,
-    merged_out,
+    schur_all,
+    merged_all,
     branching,
     sibling,
     leaf_rows,
@@ -98,6 +98,7 @@
     p_recv,
     own_sem,
     in_sem,
+    schur_out,
 ):
     leaves = ROWS_Y * ROWS_Z * CORES
     me = lax.axis_index("leaf")
@@ -365,6 +366,7 @@
             copy.wait_recv()
         schur_out[q] = half[q] + from_wire(yr[q], yr_unit[q])
         p_copy(q).start()
+        schur_all[:, q, :] = schur_out[q]
 
     reduce_x(0)
     reduce_x(1)
@@ -376,7 +378,7 @@
         p_copy(q).wait_recv()
     for q in range(2):
         choice = jnp.full((block, state), sibling[0, q], jnp.int32)
-        merged_out[q] = schur_out[q] + jnp.where(choice == 0, pr[0], pr[1])
+        merged_all[:, q, :] = schur_out[q] + jnp.where(choice == 0, pr[0], pr[1])
 
     all_weights().wait_send()
     for q in range(2):
@@ -389,10 +391,15 @@
         p_copy(q).wait_send()
 
 
-def arrange(schur, merged, schur_out, merged_out):
-    for q in range(2):
-        schur_out[:, q, :] = schur[q]
-        merged_out[:, q, :] = merged[q]
+def arrange(schur, merged, schur_out, merged_out, sem):
+    copies = [
+        pltpu.make_async_copy(schur, schur_out, sem.at[0]),
+        pltpu.make_async_copy(merged, merged_out, sem.at[1]),
+    ]
+    for copy in copies:
+        copy.start()
+    for copy in copies:
+        copy.wait()
 
 
 def shards(leaf_rows, leaf_weight, branching, sibling, node_block, na_rows, na_weight, na_route):
@@ -404,7 +411,7 @@
     dma = pltpu.SemaphoreType.DMA
     schur, merged = pl.pallas_call(
         kernel,
-        out_shape=[pltpu.VMEM((2, block, state), F32)] * 2,
+        out_shape=[pltpu.VMEM((block, 2, state), F32)] * 2,
         in_specs=[hbm] * 8,
         out_specs=[vmem, vmem],
         scratch_shapes=[
@@ -447,6 +454,7 @@
             dma((2,)),
             dma((2, 2)),
             dma((8,)),
+            pltpu.VMEM((2, block, state), F32),
         ],
         compiler_params=pltpu.CompilerParams(
             collective_id=0, has_side_effects=True, vmem_limit_bytes=60 << 20
@@ -466,7 +474,8 @@
         arrange,
         out_shape=[jax.ShapeDtypeStruct((block, 2, state), F32)] * 2,
         in_specs=[vmem, vmem],
-        out_specs=[vmem, vmem],
+        out_specs=[hbm, hbm],
+        scratch_shapes=[dma((2,))],
         name="arrange",
     )(
         pltpu.with_memory_space_constraint(schur, pltpu.VMEM),

time: 53 us -> 52.9 us (level)
  no operation moved by 1% of the time
where the time goes in v5:
time: 52.9 us; the launch traced here: 52.8 us
  Pallas kernels  52.2 us (99%)
  between operations  0.64 us (1%)
    pallas_call x1, Pallas kernels, shards(): pl.pallas_call(kernel, out_shape=[pltpu.VMEM((block, 2, state), F32)] * 2...  51.4 us

profile of v5, /device:TPU:1, one launch (start us, length us, event | category | flops | bytes accessed | tf_op | source)
XLA Modules:
  0.0 52.8 jit_solution(2237581983056152118)
XLA Ops:
  0.6 51.4 %schur_pass.1 = (f32[64,2,512]{2,1,0:T(2,128)S(1)}, f32[64,2,512]{2,1,0:T(2,128)S(1)}) custom-call(s32[2]{0:T(128)} %branching_in.1, s32[1,2]{1,0:T(1,128)} %sibling_in.1, bf16[2,8,64,512]{3,2,1,0:T(8,128)(2,1)} %leaf_rows_in.1, bf16[2,8,64]{2,1,0:T(8,128)(2,1)} %leaf_weight_in.1, bf16[64,2,512]{2,1,0:T(2,128)(2,1)} %node_block_in.1, ...), custom_call_target="tpu_custom_call" | custom-call | tf_op jit(solution)/shard_map/schur_pass/pallas_call | solution.py:412
  52.0 0.8 %arrange.1 = (f32[64,2,512]{2,1,0:T(2,128)}, f32[64,2,512]{2,1,0:T(2,128)}) custom-call(f32[64,2,512]{2,1,0:T(2,128)S(1)} %get-tuple-element.4.schur, f32[64,2,512]{2,1,0:T(2,128)S(1)} %get-tuple-element.5.merged), custom_call_target="tpu_custom_call" | custom-call | tf_op jit(solution)/shard_map/arrange/pallas_call | solution.py:473
